TPU v7x, 32 devices: a whole 2x2x4 slice. The times are simulated.
32 devices in a mesh: dp: 8 (over y, x, core), dap: 4 (over z).
Axes of the slice: x: 2, y: 2, z: 4, core: 2. Of those that a mesh axis runs over, the one named last changes fastest.
Arguments:
- pair_act: bfloat16 [8, 128, 128, 128], P('dp', 'dap'), may hold values from -6 to 6
- pair_cot: bfloat16 [8, 128, 128, 128], P('dp', 'dap'), may hold values from -6 to 6
- in_gain: float32 [128], replicated, may hold values from 0.25 to 1.75
- in_bias: float32 [128], replicated, may hold values from -3 to 3
- proj_weight: bfloat16 [128, 512], replicated, may hold values from -0.5 to 0.5
- gate_weight: bfloat16 [128, 128], replicated, may hold values from -0.5 to 0.5
- out_gain: float32 [128], replicated, may hold values from 0.25 to 1.75
- out_bias: float32 [128], replicated, may hold values from -3 to 3
- out_weight: bfloat16 [128, 128], replicated, may hold values from -0.5 to 0.5
Outputs:
- update: bfloat16 [8, 128, 128, 128], P('dp', 'dap')
- pair_grad: bfloat16 [8, 128, 128, 128], P('dp', 'dap')
- proj_grad: float32 [128, 512], replicated
- gate_grad: float32 [128, 128], replicated
- out_grad: float32 [128, 128], replicated
- in_norm_grad: float32 [2, 128], replicated
- out_norm_grad: float32 [2, 128], replicated
All inputs are finite; a program needn't handle non-finite values.
Results may differ from a plain program's by a relative error of at most 0.0084.
Values may be sent and summed in bfloat16 or wider, within the bound.
A program may use at most 64 MiB of HBM per device.

v0:
```python
import jax
import jax.numpy as jnp
from jax import lax
from jax.sharding import PartitionSpec as P

epsilon = 1e-05


def norm_rows(values, along):
    row_mean = jnp.mean(values, axis=along, keepdims=True)
    centred = values - row_mean
    row_var = jnp.mean(centred * centred, axis=along, keepdims=True)
    inv_std = lax.rsqrt(row_var + epsilon)
    return (centred * inv_std, inv_std)


def norm_back(grad_hat, x_hat, inv_std, along):
    first = jnp.mean(grad_hat, axis=along, keepdims=True)
    second = jnp.mean(grad_hat * x_hat, axis=along, keepdims=True)
    return (grad_hat - first - x_hat * second) * inv_std


def backward_pieces(piece_d, piece_l, piece_r):
    back_l = jnp.einsum(
        "zhij,zhjk->zhik", piece_d, piece_r, preferred_element_type=jnp.float32
    ).astype(jnp.bfloat16)
    back_r = jnp.einsum(
        "zhij,zhik->zhjk", piece_d, piece_l, preferred_element_type=jnp.float32
    ).astype(jnp.bfloat16)
    return (back_l, back_r)


def shards(
    pair_act, pair_cot, in_gain, in_bias, proj_weight, gate_weight, out_gain, out_bias, out_weight
):
    f32 = jnp.float32
    bf16 = jnp.bfloat16
    groups = lax.axis_size("dap")
    row_count = pair_act.shape[1]
    crop_len = pair_act.shape[2]
    channels = pair_act.shape[3]
    hidden_w = out_weight.shape[0]
    per_dev = hidden_w // groups
    cell_count = row_count * crop_len
    scale = 1.0 / crop_len
    flat_act = pair_act.reshape(cell_count, channels).astype(f32)
    in_hat, in_inv = norm_rows(flat_act, 1)
    normed = (in_hat * in_gain + in_bias).astype(bf16)
    projected = jnp.einsum("mc,ch->hm", normed, proj_weight, preferred_element_type=f32)
    pre_ag = projected[0:hidden_w]
    pre_ap = projected[hidden_w : 2 * hidden_w]
    pre_bg = projected[2 * hidden_w : 3 * hidden_w]
    pre_bp = projected[3 * hidden_w : 4 * hidden_w]
    sig_a = jax.nn.sigmoid(pre_ag)
    sig_b = jax.nn.sigmoid(pre_bg)
    left_act = (sig_a * pre_ap).astype(bf16).reshape(groups, per_dev, row_count, crop_len)
    right_act = (sig_b * pre_bp).astype(bf16).reshape(groups, per_dev, row_count, crop_len)
    piece_l = lax.all_to_all(left_act, "dap", split_axis=0, concat_axis=2, tiled=True)
    piece_r = lax.all_to_all(right_act, "dap", split_axis=0, concat_axis=2, tiled=True)
    product = jnp.einsum("zhik,zhjk->zhij", piece_l, piece_r, preferred_element_type=f32).astype(
        bf16
    )
    returned = lax.all_to_all(product, "dap", split_axis=2, concat_axis=0, tiled=True)
    tri_out = returned.reshape(hidden_w, cell_count)
    tri_hat, tri_inv = norm_rows(tri_out.astype(f32), 0)
    tri_norm = (tri_hat * out_gain[:, None] + out_bias[:, None]).astype(bf16)
    gate_val = jax.nn.sigmoid(jnp.dot(normed, gate_weight, preferred_element_type=f32))
    mixed = jnp.einsum("hm,hc->mc", tri_norm, out_weight, preferred_element_type=f32)
    update = (gate_val * mixed).astype(bf16).reshape(1, row_count, crop_len, channels)
    cot_flat = pair_cot.reshape(cell_count, channels).astype(f32)
    d_mixed = (cot_flat * gate_val).astype(bf16)
    d_gate = (cot_flat * mixed * gate_val * (1.0 - gate_val)).astype(bf16)
    out_part = jnp.einsum("hm,mc->hc", tri_norm, d_mixed, preferred_element_type=f32) * scale
    gate_part = jnp.einsum("mc,md->cd", normed, d_gate, preferred_element_type=f32) * scale
    d_norm_out = jnp.einsum("mc,hc->hm", d_mixed, out_weight, preferred_element_type=f32)
    out_norm_part = (
        jnp.stack([jnp.sum(d_norm_out * tri_hat, axis=1), jnp.sum(d_norm_out, axis=1)]) * scale
    )
    d_tri = norm_back(d_norm_out * out_gain[:, None], tri_hat, tri_inv, 0).astype(bf16)
    d_tri = d_tri.reshape(groups, per_dev, row_count, crop_len)
    d_cols = lax.all_to_all(d_tri, "dap", split_axis=0, concat_axis=2, tiled=True)
    back_l, back_r = backward_pieces(d_cols, piece_l, piece_r)
    d_left, d_right = (
        lax.all_to_all(back_l, "dap", split_axis=2, concat_axis=0, tiled=True),
        lax.all_to_all(back_r, "dap", split_axis=2, concat_axis=0, tiled=True),
    )
    left_grad = d_left.reshape(hidden_w, cell_count).astype(f32)
    right_grad = d_right.reshape(hidden_w, cell_count).astype(f32)
    d_proj = jnp.concatenate(
        [
            left_grad * pre_ap * sig_a * (1.0 - sig_a),
            left_grad * sig_a,
            right_grad * pre_bp * sig_b * (1.0 - sig_b),
            right_grad * sig_b,
        ],
        axis=0,
    ).astype(bf16)
    proj_part = jnp.einsum("mc,hm->ch", normed, d_proj, preferred_element_type=f32) * scale
    d_normed = jnp.einsum(
        "hm,ch->mc", d_proj, proj_weight, preferred_element_type=f32
    ) + jnp.einsum("md,cd->mc", d_gate, gate_weight, preferred_element_type=f32)
    in_norm_part = (
        jnp.stack([jnp.sum(d_normed * in_hat, axis=0), jnp.sum(d_normed, axis=0)]) * scale
    )
    pair_grad = (
        norm_back(d_normed * in_gain, in_hat, in_inv, 1)
        .astype(bf16)
        .reshape(1, row_count, crop_len, channels)
    )
    proj_sum, gate_sum, out_sum, in_sum, outn_sum = lax.psum(
        (proj_part, gate_part, out_part, in_norm_part, out_norm_part), ("dp", "dap")
    )
    return (update, pair_grad, proj_sum, gate_sum, out_sum, in_sum, outn_sum)


def solution(mesh):
    placed = (
        P("dp", "dap", None, None),
        P("dp", "dap", None, None),
        P(),
        P(),
        P(),
        P(),
        P(),
        P(),
        P(),
    )
    return jax.shard_map(
        shards,
        mesh=mesh,
        in_specs=placed,
        out_specs=(P("dp", "dap", None, None), P("dp", "dap", None, None), P(), P(), P(), P(), P()),
        check_vma=False,
    )
```

profile of v0, /device:TPU:0, one launch (start us, length us, event | category | flops | bytes accessed | tf_op | source)
XLA Modules:
  0.0 383.8 jit_solution(13851624344998094155)
XLA Ops:
  7.2 1.7 convert_reduce_fusion
  8.9 2.3 multiply_reduce_fusion.3
  11.3 1.3 add_convert_fusion.1
  12.6 1.0 copy-done.5
  13.5 1.3 convolution_bitcast_fusion
  14.8 1.1 fusion.30
  15.9 2.1 copy-done.1
  18.1 1.2 copy.46
  19.3 6.3 %all-to-all-start.1 = ((bf16[4,32,32,128]{3,2,1,0:T(8,128)(2,1)}), bf16[4,32,32,128]{3,2,1,0:T(8,128)(2,1)S(1)}, u32[]{:S(2)}, u32[]{:S(2)}) async-start(bf16[4,32,32,128]{3,2,1,0:T(8,128)(2,1)} %bitcast.157), calls=%async_computation.1 | async-start | bytes 2097152 | tf_op jit(solution)/shard_map/all_to_all | solution.py:59
  25.6 1.2 copy.45
  26.8 24.5 %all-to-all-done.1 = bf16[4,32,32,128]{3,2,1,0:T(8,128)(2,1)S(1)} async-done(((bf16[4,32,32,128]{3,2,1,0:T(8,128)(2,1)}), bf16[4,32,32,128]{3,2,1,0:T(8,128)(2,1)S(1)}, u32[]{:S(2)}, u32[]{:S(2)}) %all-to-all-start.1) | async-done | bytes 1048608 | tf_op jit(solution)/shard_map/all_to_all | solution.py:59
  51.4 4.3 %all-to-all-start = ((bf16[4,32,32,128]{3,2,1,0:T(8,128)(2,1)}), bf16[4,32,32,128]{3,2,1,0:T(8,128)(2,1)}, u32[]{:S(2)}, u32[]{:S(2)}) async-start(bf16[4,32,32,128]{3,2,1,0:T(8,128)(2,1)} %bitcast.156), calls=%async_computation | async-start | bytes 2097152 | tf_op jit(solution)/shard_map/all_to_all | solution.py:58
  55.8 25.2 %all-to-all-done = bf16[4,32,32,128]{3,2,1,0:T(8,128)(2,1)} async-done(((bf16[4,32,32,128]{3,2,1,0:T(8,128)(2,1)}), bf16[4,32,32,128]{3,2,1,0:T(8,128)(2,1)}, u32[]{:S(2)}, u32[]{:S(2)}) %all-to-all-start) | async-done | bytes 1048608 | tf_op jit(solution)/shard_map/all_to_all | solution.py:58
  81.0 1.3 copy.32
  83.9 27.7 %all_to_all.72 = bf16[1,32,128,128]{3,1,0,2:T(8,128)(2,1)S(1)} all-to-all(bf16[1,32,128,128]{3,1,0,2:T(8,128)(2,1)S(1)} %copy.34), channel_id=1, replica_groups=mesh['dp'=8,'dap'=4] {'dap'}, dimensions={2} | all-to-all | bytes 2097152 | tf_op jit(solution)/shard_map/all_to_all | solution.py:63
  112.2 1.1 bitcast_reduce_fusion
  113.4 1.1 fusion.23
  114.5 3.0 copy.58
  117.5 1.9 copy.36
  119.4 2.3 add_convert_fusion
  121.8 1.0 copy-done.12
  124.3 2.7 fusion.6
  127.0 2.4 fusion.21
  129.4 1.3 copy-done.3
  130.8 4.1 %multiply_convert_fusion.1 = bf16[128,4096]{0,1:T(8,128)(2,1)} fusion(f32[4096,128]{1,0:T(8,128)S(1)} %get-tuple-element.34, f32[128,4096]{0,1:T(8,128)S(1)} %copy.36, f32[4096]{0:T(1024)S(1)} %get-tuple-element.36, f32[4096]{0:T(1024)S(1)} %get-tuple-element.37, f32[128]{0:T(128)S(1)} %copy-done.22, f32[4096]{0:T(1024)S(1)} %rsqrt_bitcast_fusion, ...), kind=kLoop, calls=%fused_computation.46 | loop fusion | flops 4194304 | bytes 5308928 | tf_op jit(solution)/shard_map/convert_element_type | solution.py:79
  134.8 1.5 copy.37
  136.6 27.8 %all_to_all.73 = bf16[4,32,32,128]{3,2,1,0:T(8,128)(2,1)S(1)} all-to-all(bf16[4,32,32,128]{3,2,1,0:T(8,128)(2,1)S(1)} %bitcast.159), channel_id=1, replica_groups=mesh['dp'=8,'dap'=4] {'dap'}, dimensions={0} | all-to-all | bytes 2097152 | tf_op jit(solution)/shard_map/all_to_all | solution.py:81
  165.0 1.7 copy.39
  166.6 4.3 %all-to-all-start.4 = ((bf16[1,32,128,128]{3,1,0,2:T(8,128)(2,1)}), bf16[1,32,128,128]{3,1,0,2:T(8,128)(2,1)}, u32[]{:S(2)}, u32[]{:S(2)}) async-start(bf16[1,32,128,128]{3,1,0,2:T(8,128)(2,1)} %copy.39), calls=%async_computation.4 | async-start | bytes 2097152 | tf_op jit(solution)/shard_map/all_to_all | solution.py:84
  171.4 1.7 copy.42
  173.1 22.6 %all-to-all-done.4 = bf16[1,32,128,128]{3,1,0,2:T(8,128)(2,1)} async-done(((bf16[1,32,128,128]{3,1,0,2:T(8,128)(2,1)}), bf16[1,32,128,128]{3,1,0,2:T(8,128)(2,1)}, u32[]{:S(2)}, u32[]{:S(2)}) %all-to-all-start.4) | async-done | bytes 1048608 | tf_op jit(solution)/shard_map/all_to_all | solution.py:84
  195.7 4.5 %all-to-all-start.5 = ((bf16[1,32,128,128]{3,1,0,2:T(8,128)(2,1)}), bf16[1,32,128,128]{3,1,0,2:T(8,128)(2,1)}, u32[]{:S(2)}, u32[]{:S(2)}) async-start(bf16[1,32,128,128]{3,1,0,2:T(8,128)(2,1)} %copy.42), calls=%async_computation.5 | async-start | bytes 2097152 | tf_op jit(solution)/shard_map/all_to_all | solution.py:85
  200.8 2.8 convolution_multiply_fusion.1
  203.6 1.1 convolution_multiply_fusion.2
  204.7 2.9 copy.40
  207.7 17.9 %all-to-all-done.5 = bf16[1,32,128,128]{3,1,0,2:T(8,128)(2,1)} async-done(((bf16[1,32,128,128]{3,1,0,2:T(8,128)(2,1)}), bf16[1,32,128,128]{3,1,0,2:T(8,128)(2,1)}, u32[]{:S(2)}, u32[]{:S(2)}) %all-to-all-start.5) | async-done | bytes 1048608 | tf_op jit(solution)/shard_map/all_to_all | solution.py:85
  225.5 1.7 copy.43
  227.4 6.3 %fusion.13 = (bf16[128,4096]{1,0:T(8,128)(2,1)S(1)}, bf16[128,4096]{1,0:T(8,128)(2,1)S(1)}, bf16[128,4096]{1,0:T(8,128)(2,1)S(1)}, bf16[128,4096]{1,0:T(8,128)(2,1)S(1)}) fusion(f32[16,8,32,128]{3,2,1,0:T(8,128)S(1)} %bitcast.153, f32[512,4096]{1,0:T(8,128)} %copy-done.1, f32[16,8,32,128]{3,2,1,0:T(8,128)S(1)} %bitcast.154), kind=kLoop, calls=%fused_computation.23 | loop fusion | flops 10485760 | bytes 16777216 | tf_op jit(solution)/shard_map/convert.13
  233.8 1.0 copy-done.17
  235.4 2.2 convolution_multiply_fusion
  237.6 3.0 fusion.31
  240.6 2.4 multiply_reduce_fusion
  243.1 3.3 multiply_convert_fusion
  246.3 37.9 %all-reduce = (f32[2,128]{1,0:T(2,128)}, f32[2,128]{1,0:T(2,128)}) all-reduce(f32[2,128]{1,0:T(2,128)S(1)} %maximum_multiply_fusion, f32[2,128]{1,0:T(2,128)S(1)} %maximum_multiply_fusion.1), channel_id=1, replica_groups=mesh['dp'=8,'dap'=4] {'dp','dap'}, use_global_device_ids=true, to_apply=%region_13.0 | all-reduce | flops 512 | bytes 4096 | tf_op jit(solution)/shard_map/psum | solution.py:110
  284.3 88.0 %all-reduce.4.cloned.1.call-done = (f32[128,512]{1,0:T(8,128)}, f32[128,128]{1,0:T(8,128)}, f32[128,128]{1,0:T(8,128)}) async-done(((f32[128,512]{1,0:T(8,128)}, f32[128,128]{1,0:T(8,128)}, f32[128,128]{1,0:T(8,128)}), (f32[128,512]{1,0:T(8,128)}, f32[128,128]{1,0:T(8,128)}, f32[128,128]{1,0:T(8,128)})) %all-reduce.4.cloned.1.call-update) | async-done | bytes 393232 | tf_op jit(solution)/shard_map/psum | solution.py:110
  372.3 1.7 copy.62
  374.0 1.5 copy.63
  375.5 1.5 copy.64
  (71 shorter events, 6.8 us)
Async XLA Ops:
  7.2 6.4 %copy-start = (bf16[128,512]{1,0:T(8,128)(2,1)S(1)}, bf16[128,512]{1,0:T(8,128)(2,1)}, u32[]{:S(2)}) copy-start(bf16[128,512]{1,0:T(8,128)(2,1)} %param.13) | copy-start | bytes 393220
  7.2 4.1 %copy-start.2 = (bf16[1,32,128,128]{3,2,1,0:T(8,128)(2,1)S(1)}, bf16[1,32,128,128]{3,2,1,0:T(8,128)(2,1)}, u32[]{:S(2)}) copy-start(bf16[1,32,128,128]{3,2,1,0:T(8,128)(2,1)} %param.9) | copy-start | bytes 3145732
  7.2 4.1 %copy-start.23 = (f32[128]{0:T(128)S(1)}, f32[128]{0:T(128)}, u32[]{:S(2)}) copy-start(f32[128]{0:T(128)} %param.11) | copy-start | bytes 1540
  7.2 4.1 %copy-start.25 = (f32[128]{0:T(128)S(1)}, f32[128]{0:T(128)}, u32[]{:S(2)}) copy-start(f32[128]{0:T(128)} %param.12) | copy-start | bytes 1540
  12.6 1.0 copy-start.5
  14.8 3.2 copy-start.1
  19.3 32.1 %all-to-all-start.1 = ((bf16[4,32,32,128]{3,2,1,0:T(8,128)(2,1)}), bf16[4,32,32,128]{3,2,1,0:T(8,128)(2,1)S(1)}, u32[]{:S(2)}, u32[]{:S(2)}) async-start(bf16[4,32,32,128]{3,2,1,0:T(8,128)(2,1)} %bitcast.157), calls=%async_computation.1 | async-start | bytes 2097152 | tf_op jit(solution)/shard_map/all_to_all | solution.py:59
  51.4 29.6 %all-to-all-start = ((bf16[4,32,32,128]{3,2,1,0:T(8,128)(2,1)}), bf16[4,32,32,128]{3,2,1,0:T(8,128)(2,1)}, u32[]{:S(2)}, u32[]{:S(2)}) async-start(bf16[4,32,32,128]{3,2,1,0:T(8,128)(2,1)} %bitcast.156), calls=%async_computation | async-start | bytes 2097152 | tf_op jit(solution)/shard_map/all_to_all | solution.py:58
  55.8 27.4 %copy-start.10 = (bf16[1,32,4,32,128]{4,3,2,1,0:T(8,128)(2,1)}, bf16[1,32,4,32,128]{4,3,2,1,0:T(8,128)(2,1)S(1)}, u32[]{:S(2)}) copy-start(bf16[1,32,4,32,128]{4,3,2,1,0:T(8,128)(2,1)S(1)} %copy.33) | copy-start | bytes 3145732
  82.3 1.6 copy-start.8
  117.5 2.0 copy-start.22
  117.5 2.0 copy-start.24
  119.4 3.3 copy-start.20
  121.7 1.0 copy-start.12
  122.7 1.2 copy-start.6
  122.7 1.2 copy-start.21
  122.8 1.6 copy-start.26
  127.0 2.4 copy-start.16
  129.4 1.4 copy-start.3
  136.6 27.9 %copy-start.11 = (bf16[1,32,4,32,128]{4,3,2,1,0:T(8,128)(2,1)S(1)}, bf16[1,32,4,32,128]{4,3,2,1,0:T(8,128)(2,1)}, u32[]{:S(2)}) copy-start(bf16[1,32,4,32,128]{4,3,2,1,0:T(8,128)(2,1)} %copy-done.10) | copy-start | bytes 3145732
  165.0 5.9 %copy-start.9 = (bf16[1,32,4,32,128]{4,3,2,1,0:T(8,128)(2,1)S(1)}, bf16[1,32,4,32,128]{4,3,2,1,0:T(8,128)(2,1)}, u32[]{:S(2)}) copy-start(bf16[1,32,4,32,128]{4,3,2,1,0:T(8,128)(2,1)} %copy-done.8) | copy-start | bytes 3145732
  166.6 29.1 %all-to-all-start.4 = ((bf16[1,32,128,128]{3,1,0,2:T(8,128)(2,1)}), bf16[1,32,128,128]{3,1,0,2:T(8,128)(2,1)}, u32[]{:S(2)}, u32[]{:S(2)}) async-start(bf16[1,32,128,128]{3,1,0,2:T(8,128)(2,1)} %copy.39), calls=%async_computation.4 | async-start | bytes 2097152 | tf_op jit(solution)/shard_map/all_to_all | solution.py:84
  171.4 28.8 %copy-start.4 = (f32[4096,128]{1,0:T(8,128)S(1)}, f32[4096,128]{1,0:T(8,128)}, u32[]{:S(2)}) copy-start(f32[4096,128]{1,0:T(8,128)} %copy-done.3) | copy-start | bytes 6291460
  195.7 29.8 %all-to-all-start.5 = ((bf16[1,32,128,128]{3,1,0,2:T(8,128)(2,1)}), bf16[1,32,128,128]{3,1,0,2:T(8,128)(2,1)}, u32[]{:S(2)}, u32[]{:S(2)}) async-start(bf16[1,32,128,128]{3,1,0,2:T(8,128)(2,1)} %copy.42), calls=%async_computation.5 | async-start | bytes 2097152 | tf_op jit(solution)/shard_map/all_to_all | solution.py:85
  200.2 172.1 %all-reduce.4.cloned.1.call-start = ((), (), s32[]{:S(2)}) async-start(), calls=%async_computation.6 | async-start | bytes 786432 | tf_op jit(solution)/shard_map/psum | solution.py:110
  200.8 2.8 copy-start.7
  200.8 2.8 copy-start.14
  225.5 1.9 copy-start.13
  233.7 1.0 copy-start.17
  233.8 1.3 copy-start.18
  233.8 1.6 copy-start.19
  237.6 3.0 copy-start.15
Sparse Core Ops, SparseCore 0:
  243.2 129.0 all-reduce.3
where the time goes:
time: 385 us; the launch traced here: 384 us
  waiting for transfers between devices  178 us (46%)
  blocking collectives  93.5 us (24%)
  local copies, waits for them, and re-layouts  32.7 us (8%)
  other arithmetic  25.3 us (7%)
  matrix products  20.1 us (5%)
  starting transfers between devices  19.4 us (5%)
  between operations  14.6 us (4%)
    psum x1, waiting for transfers between devices, shards(): lax.psum((proj_part, gate_part, out_part, in_norm_part, out_norm_part), (...  88 us
    psum x1, blocking collectives, shards(): lax.psum((proj_part, gate_part, out_part, in_norm_part, out_norm_part), (...  37.9 us
    all_to_all x1, blocking collectives, shards(): lax.all_to_all(d_tri, 'dap', split_axis=0, concat_axis=2, tiled=True)  27.8 us
    all_to_all x1, blocking collectives, shards(): lax.all_to_all(product, 'dap', split_axis=2, concat_axis=0, tiled=True)  27.7 us
    all_to_all x1, waiting for transfers between devices, shards(): lax.all_to_all(left_act, 'dap', split_axis=0, concat_axis=2, tiled=True)  25.2 us
    all_to_all x1, waiting for transfers between devices, shards(): lax.all_to_all(right_act, 'dap', split_axis=0, concat_axis=2, tiled=True)  24.5 us
    all_to_all x1, waiting for transfers between devices, shards(): lax.all_to_all(back_l, 'dap', split_axis=2, concat_axis=0, tiled=True)  22.6 us
    unnamed x61, local copies, waits for them, and re-layouts  18.7 us
  transfers between devices with their start and end apart: 5, of which 5 were waited for; matrix products, arithmetic and copies ran while one was open for 4% of the time, Pallas kernels for 0%

commit v1 on v0

--- a/solution.py
+++ b/solution.py
@@ -4,6 +4,30 @@
 from jax.sharding import PartitionSpec as P
 
 epsilon = 1e-05
+
+
+def cut_along(array, dim, size):
+    lengths = array.shape
+    tiles = array.reshape(*lengths[:dim], size, lengths[dim] // size, *lengths[dim + 1 :])
+    return jnp.moveaxis(tiles, dim, 0)
+
+
+def joined_along(blocks, dim):
+    blocks = jnp.moveaxis(blocks, 0, dim)
+    dims = blocks.shape
+    return blocks.reshape(*dims[:dim], dims[dim] * dims[dim + 1], *dims[dim + 2 :])
+
+
+def sent_to_each(x, axis, split_dim, concat_dim):
+    size, position = (lax.axis_size(axis), lax.axis_index(axis))
+    pieces = cut_along(x, split_dim, size)
+    out = pieces
+    for step in range(1, size):
+        target, source = ((position + step) % size, (position - step) % size)
+        sent = lax.dynamic_index_in_dim(pieces, target, 0)
+        other = lax.ppermute(sent, axis, [(i, (i + step) % size) for i in range(size)])
+        out = lax.dynamic_update_slice_in_dim(out, other, source, axis=0)
+    return joined_along(out, concat_dim)
 
 
 def norm_rows(values, along):
@@ -60,7 +84,7 @@
     product = jnp.einsum("zhik,zhjk->zhij", piece_l, piece_r, preferred_element_type=f32).astype(
         bf16
     )
-    returned = lax.all_to_all(product, "dap", split_axis=2, concat_axis=0, tiled=True)
+    returned = sent_to_each(product, "dap", 2, 0)
     tri_out = returned.reshape(hidden_w, cell_count)
     tri_hat, tri_inv = norm_rows(tri_out.astype(f32), 0)
     tri_norm = (tri_hat * out_gain[:, None] + out_bias[:, None]).astype(bf16)

time: 385 us -> 379 us (0.984)
  blocking collectives: 93.5 us -> 69.5 us
  waiting for transfers between devices: 178 us -> 192 us
    all_to_all x1 -> x0, blocking collectives: 27.7 us -> none  [shards(): lax.all_to_all(product, 'dap', split_axis=2, concat_axis=0, tiled=True)]
    ppermute x0 -> x3, waiting for transfers between devices: none -> 17.2 us  [sent_to_each(): lax.ppermute(sent, axis, [(i, (i + step) % size) for i in range(size)])]
  transfers between devices with their start and end apart: 5 -> 8, of which waited for: 5 -> 7; matrix products, arithmetic and copies ran while one was open for 4% -> 6% of each run, Pallas kernels for 0% -> 0%
where the time goes in v1:
time: 379 us; the launch traced here: 378 us
  waiting for transfers between devices  192 us (51%)
  blocking collectives  69.5 us (18%)
  local copies, waits for them, and re-layouts  34 us (9%)
  other arithmetic  25 us (7%)
  matrix products  22.4 us (6%)
  starting transfers between devices  20.4 us (5%)
  between operations  14.6 us (4%)
    psum x1, waiting for transfers between devices, shards(): lax.psum((proj_part, gate_part, out_part, in_norm_part, out_norm_part), (...  86.6 us
    psum x1, blocking collectives, shards(): lax.psum((proj_part, gate_part, out_part, in_norm_part, out_norm_part), (...  37.9 us
    all_to_all x1, blocking collectives, shards(): lax.all_to_all(d_tri, 'dap', split_axis=0, concat_axis=2, tiled=True)  31.6 us
    all_to_all x1, waiting for transfers between devices, shards(): lax.all_to_all(right_act, 'dap', split_axis=0, concat_axis=2, tiled=True)  24.6 us
    all_to_all x1, waiting for transfers between devices, shards(): lax.all_to_all(back_l, 'dap', split_axis=2, concat_axis=0, tiled=True)  23.1 us
    all_to_all x1, waiting for transfers between devices, shards(): lax.all_to_all(left_act, 'dap', split_axis=0, concat_axis=2, tiled=True)  22.9 us
    all_to_all x1, waiting for transfers between devices, shards(): lax.all_to_all(back_r, 'dap', split_axis=2, concat_axis=0, tiled=True)  17.9 us
    ppermute x3, waiting for transfers between devices, sent_to_each(): lax.ppermute(sent, axis, [(i, (i + step) % size) for i in range(size)])  17.2 us
  transfers between devices with their start and end apart: 8, of which 7 were waited for; matrix products, arithmetic and copies ran while one was open for 6% of the time, Pallas kernels for 0%

profile of v1, /device:TPU:0, one launch (start us, length us, event | category | flops | bytes accessed | tf_op | source)
XLA Modules:
  0.0 378.3 jit_solution(1075280760109512975)
XLA Ops:
  7.2 1.7 convert_reduce_fusion
  8.9 2.3 multiply_reduce_fusion.4
  11.3 1.3 add_convert_fusion.1
  12.6 1.3 convolution_bitcast_fusion
  13.9 1.1 fusion.27
  15.0 2.1 copy-done.1
  17.1 1.2 copy.45
  18.3 6.3 %all-to-all-start.1 = ((bf16[4,32,32,128]{3,2,1,0:T(8,128)(2,1)}), bf16[4,32,32,128]{3,2,1,0:T(8,128)(2,1)}, u32[]{:S(2)}, u32[]{:S(2)}) async-start(bf16[4,32,32,128]{3,2,1,0:T(8,128)(2,1)} %bitcast.158), calls=%async_computation.1 | async-start | bytes 2097152 | tf_op jit(solution)/shard_map/all_to_all | solution.py:83
  24.6 1.2 copy.44
  25.8 24.6 %all-to-all-done.1 = bf16[4,32,32,128]{3,2,1,0:T(8,128)(2,1)} async-done(((bf16[4,32,32,128]{3,2,1,0:T(8,128)(2,1)}), bf16[4,32,32,128]{3,2,1,0:T(8,128)(2,1)}, u32[]{:S(2)}, u32[]{:S(2)}) %all-to-all-start.1) | async-done | bytes 1048608 | tf_op jit(solution)/shard_map/all_to_all | solution.py:83
  50.5 3.5 all-to-all-start
  54.0 2.3 copy.33
  56.4 22.9 %all-to-all-done = bf16[4,32,32,128]{3,2,1,0:T(8,128)(2,1)S(1)} async-done(((bf16[4,32,32,128]{3,2,1,0:T(8,128)(2,1)}), bf16[4,32,32,128]{3,2,1,0:T(8,128)(2,1)S(1)}, u32[]{:S(2)}, u32[]{:S(2)}) %all-to-all-start) | async-done | bytes 1048608 | tf_op jit(solution)/shard_map/all_to_all | solution.py:82
  79.4 1.5 copy-done.9
  82.6 1.5 collective-permute-start.2
  84.6 2.1 fusion.2
  86.8 13.9 %collective-permute-done = bf16[1,1,32,32,128]{4,3,2,0,1:T(8,128)(2,1)} collective-permute-done((bf16[1,1,32,32,128]{4,3,2,0,1:T(8,128)(2,1)}, bf16[1,1,32,32,128]{4,3,2,0,1:T(8,128)(2,1)}, u32[]{:S(2)}, u32[]{:S(2)}) %collective-permute-start) | collective-permute-done | bytes 262176 | tf_op jit(solution)/shard_map/ppermute | solution.py:28
  101.7 3.4 collective-permute-done.1
  106.0 1.0 constant_dynamic-update-slice_fusion
  107.5 1.7 copy.56
  109.3 1.9 copy.35
  111.3 2.3 add_convert_fusion
  113.6 2.2 fusion.6
  115.8 2.5 fusion.21
  118.3 1.3 copy-done.3
  119.7 4.1 %multiply_convert_fusion.1 = bf16[128,4096]{0,1:T(8,128)(2,1)} fusion(f32[4096,128]{1,0:T(8,128)S(1)} %get-tuple-element.37, f32[128,4096]{0,1:T(8,128)S(1)} %copy.35, f32[4096]{0:T(1024)S(1)} %get-tuple-element.39, f32[4096]{0:T(1024)S(1)} %get-tuple-element.40, f32[128]{0:T(128)S(1)} %copy-done.23, f32[4096]{0:T(1024)S(1)} %rsqrt_bitcast_fusion, ...), kind=kLoop, calls=%fused_computation.42 | loop fusion | flops 4194304 | bytes 5308928 | tf_op jit(solution)/shard_map/convert_element_type | solution.py:103
  123.8 1.5 copy.36
  125.5 31.6 %all_to_all.63 = bf16[4,32,32,128]{3,2,1,0:T(8,128)(2,1)S(1)} all-to-all(bf16[4,32,32,128]{3,2,1,0:T(8,128)(2,1)S(1)} %bitcast.160), channel_id=1, replica_groups=mesh['dp'=8,'dap'=4] {'dap'}, dimensions={0} | all-to-all | bytes 2097152 | tf_op jit(solution)/shard_map/all_to_all | solution.py:105
  157.7 1.6 copy.38
  159.4 4.3 %all-to-all-start.3 = ((bf16[1,32,128,128]{3,1,0,2:T(8,128)(2,1)}), bf16[1,32,128,128]{3,1,0,2:T(8,128)(2,1)}, u32[]{:S(2)}, u32[]{:S(2)}) async-start(bf16[1,32,128,128]{3,1,0,2:T(8,128)(2,1)} %copy.38), calls=%async_computation.3 | async-start | bytes 2097152 | tf_op jit(solution)/shard_map/all_to_all | solution.py:108
  164.2 1.7 copy.41
  165.8 23.1 %all-to-all-done.3 = bf16[1,32,128,128]{3,1,0,2:T(8,128)(2,1)} async-done(((bf16[1,32,128,128]{3,1,0,2:T(8,128)(2,1)}), bf16[1,32,128,128]{3,1,0,2:T(8,128)(2,1)}, u32[]{:S(2)}, u32[]{:S(2)}) %all-to-all-start.3) | async-done | bytes 1048608 | tf_op jit(solution)/shard_map/all_to_all | solution.py:108
  189.0 4.3 %all-to-all-start.4 = ((bf16[1,32,128,128]{3,1,0,2:T(8,128)(2,1)}), bf16[1,32,128,128]{3,1,0,2:T(8,128)(2,1)}, u32[]{:S(2)}, u32[]{:S(2)}) async-start(bf16[1,32,128,128]{3,1,0,2:T(8,128)(2,1)} %copy.41), calls=%async_computation.4 | async-start | bytes 2097152 | tf_op jit(solution)/shard_map/all_to_all | solution.py:109
  193.9 2.8 convolution_multiply_fusion.1
  196.7 1.1 convolution_multiply_fusion.2
  197.8 2.9 copy.39
  200.7 17.9 %all-to-all-done.4 = bf16[1,32,128,128]{3,1,0,2:T(8,128)(2,1)} async-done(((bf16[1,32,128,128]{3,1,0,2:T(8,128)(2,1)}), bf16[1,32,128,128]{3,1,0,2:T(8,128)(2,1)}, u32[]{:S(2)}, u32[]{:S(2)}) %all-to-all-start.4) | async-done | bytes 1048608 | tf_op jit(solution)/shard_map/all_to_all | solution.py:109
  218.6 1.7 copy.42
  220.5 6.3 %fusion.13 = (bf16[128,4096]{1,0:T(8,128)(2,1)S(1)}, bf16[128,4096]{1,0:T(8,128)(2,1)S(1)}, bf16[128,4096]{1,0:T(8,128)(2,1)S(1)}, bf16[128,4096]{1,0:T(8,128)(2,1)S(1)}) fusion(f32[16,8,32,128]{3,2,1,0:T(8,128)S(1)} %bitcast.152, f32[512,4096]{1,0:T(8,128)} %copy-done.1, f32[16,8,32,128]{3,2,1,0:T(8,128)S(1)} %bitcast.153), kind=kLoop, calls=%fused_computation.23 | loop fusion | flops 10485760 | bytes 16777216 | tf_op jit(solution)/shard_map/convert.9
  228.8 2.2 convolution_multiply_fusion
  231.0 3.0 fusion.28
  234.1 3.4 multiply_reduce_fusion
  237.5 4.8 %multiply_convert_fusion = bf16[4096,128]{1,0:T(8,128)(2,1)} fusion(f32[4096,128]{1,0:T(8,128)} %get-tuple-element.38, bf16[1,32,128,128]{3,2,1,0:T(8,128)(2,1)S(1)} %copy-done.2, f32[4096]{0:T(1024)S(1)} %broadcast_multiply_fusion, f32[4096]{0:T(1024)S(1)} %broadcast_multiply_fusion.1, f32[128]{0:T(128)S(1)} %copy-done.24, ...), kind=kLoop, calls=%fused_computation.40 | loop fusion | flops 4718592 | bytes 4260352 | tf_op jit(solution)/shard_map/convert_element_type | solution.py:131
  242.3 37.9 %all-reduce = (f32[2,128]{1,0:T(2,128)}, f32[2,128]{1,0:T(2,128)}) all-reduce(f32[2,128]{1,0:T(2,128)S(1)} %maximum_multiply_fusion, f32[2,128]{1,0:T(2,128)S(1)} %maximum_multiply_fusion.1), channel_id=1, replica_groups=mesh['dp'=8,'dap'=4] {'dp','dap'}, use_global_device_ids=true, to_apply=%region_13.14 | all-reduce | flops 512 | bytes 4096 | tf_op jit(solution)/shard_map/psum | solution.py:134
  280.2 86.6 %all-reduce.4.cloned.1.call-done = (f32[128,512]{1,0:T(8,128)}, f32[128,128]{1,0:T(8,128)}, f32[128,128]{1,0:T(8,128)}) async-done(((f32[128,512]{1,0:T(8,128)}, f32[128,128]{1,0:T(8,128)}, f32[128,128]{1,0:T(8,128)}), (f32[128,512]{1,0:T(8,128)}, f32[128,128]{1,0:T(8,128)}, f32[128,128]{1,0:T(8,128)})) %all-reduce.4.cloned.1.call-update) | async-done | bytes 393232 | tf_op jit(solution)/shard_map/psum | solution.py:134
  366.8 1.7 copy.64
  368.5 1.5 copy.65
  369.9 1.5 copy.66
  (78 shorter events, 9.2 us)
Async XLA Ops:
  7.2 5.4 %copy-start = (bf16[128,512]{1,0:T(8,128)(2,1)S(1)}, bf16[128,512]{1,0:T(8,128)(2,1)}, u32[]{:S(2)}) copy-start(bf16[128,512]{1,0:T(8,128)(2,1)} %param.13) | copy-start | bytes 393220
  7.2 4.1 %copy-start.2 = (bf16[1,32,128,128]{3,2,1,0:T(8,128)(2,1)S(1)}, bf16[1,32,128,128]{3,2,1,0:T(8,128)(2,1)}, u32[]{:S(2)}) copy-start(bf16[1,32,128,128]{3,2,1,0:T(8,128)(2,1)} %param.9) | copy-start | bytes 3145732
  7.2 4.1 %copy-start.24 = (f32[128]{0:T(128)S(1)}, f32[128]{0:T(128)}, u32[]{:S(2)}) copy-start(f32[128]{0:T(128)} %param.11) | copy-start | bytes 1540
  7.2 4.1 %copy-start.26 = (f32[128]{0:T(128)S(1)}, f32[128]{0:T(128)}, u32[]{:S(2)}) copy-start(f32[128]{0:T(128)} %param.12) | copy-start | bytes 1540
  12.6 72.1 %copy-start.5 = (bf16[4096,128]{1,0:T(8,128)(2,1)}, bf16[4096,128]{1,0:T(8,128)(2,1)S(1)}, u32[]{:S(2)}) copy-start(bf16[4096,128]{1,0:T(8,128)(2,1)S(1)} %add_convert_fusion.1) | copy-start | bytes 3145732
  13.9 3.2 copy-start.1
  18.3 32.2 %all-to-all-start.1 = ((bf16[4,32,32,128]{3,2,1,0:T(8,128)(2,1)}), bf16[4,32,32,128]{3,2,1,0:T(8,128)(2,1)}, u32[]{:S(2)}, u32[]{:S(2)}) async-start(bf16[4,32,32,128]{3,2,1,0:T(8,128)(2,1)} %bitcast.158), calls=%async_computation.1 | async-start | bytes 2097152 | tf_op jit(solution)/shard_map/all_to_all | solution.py:83
  50.5 28.8 %all-to-all-start = ((bf16[4,32,32,128]{3,2,1,0:T(8,128)(2,1)}), bf16[4,32,32,128]{3,2,1,0:T(8,128)(2,1)S(1)}, u32[]{:S(2)}, u32[]{:S(2)}) async-start(bf16[4,32,32,128]{3,2,1,0:T(8,128)(2,1)} %bitcast.156), calls=%async_computation | async-start | bytes 2097152 | tf_op jit(solution)/shard_map/all_to_all | solution.py:82
  79.2 1.6 copy-start.9
  79.4 3.2 copy-start.7
  80.9 3.8 %copy-start.22 = (bf16[128,128]{1,0:T(8,128)(2,1)S(1)}, bf16[128,128]{1,0:T(8,128)(2,1)}, u32[]{:S(2)}) copy-start(bf16[128,128]{1,0:T(8,128)(2,1)} %param.14) | copy-start | bytes 98308
  82.6 23.4 %collective-permute-start.2 = (bf16[1,1,32,32,128]{4,3,2,0,1:T(8,128)(2,1)}, bf16[1,1,32,32,128]{4,3,2,0,1:T(8,128)(2,1)}, u32[]{:S(2)}, u32[]{:S(2)}) collective-permute-start(bf16[1,1,32,32,128]{4,3,2,0,1:T(8,128)(2,1)} %get-tuple-element.30), channel_id=1, source_target_pairs={{0,3},{1,0},{2,1},{3,2},{4,7},{5,4},{6,5},{7,6},{8,11},{9,8},{10,9... | collective-permute-start | bytes 786440 | tf_op jit(solution)/shard_map/ppermute | solution.py:28
  84.1 20.9 %collective-permute-start.1 = (bf16[1,1,32,32,128]{4,3,2,0,1:T(8,128)(2,1)}, bf16[1,1,32,32,128]{4,3,2,0,1:T(8,128)(2,1)}, u32[]{:S(2)}, u32[]{:S(2)}) collective-permute-start(bf16[1,1,32,32,128]{4,3,2,0,1:T(8,128)(2,1)} %get-tuple-element.31), channel_id=1, source_target_pairs={{0,2},{1,3},{2,0},{3,1},{4,6},{5,7},{6,4},{7,5},{8,10},{9,11},{10,... | collective-permute-start | bytes 786440 | tf_op jit(solution)/shard_map/ppermute | solution.py:28
  84.1 16.6 %collective-permute-start = (bf16[1,1,32,32,128]{4,3,2,0,1:T(8,128)(2,1)}, bf16[1,1,32,32,128]{4,3,2,0,1:T(8,128)(2,1)}, u32[]{:S(2)}, u32[]{:S(2)}) collective-permute-start(bf16[1,1,32,32,128]{4,3,2,0,1:T(8,128)(2,1)} %get-tuple-element.32), channel_id=1, source_target_pairs={{0,1},{1,2},{2,3},{3,0},{4,5},{5,6},{6,7},{7,4},{8,9},{9,10},{10,1... | collective-permute-start | bytes 786440 | tf_op jit(solution)/shard_map/ppermute | solution.py:28
  109.3 2.0 copy-start.23
  109.3 2.0 copy-start.25
  111.2 2.4 copy-start.15
  111.2 2.4 copy-start.16
  111.2 2.4 copy-start.21
  113.6 2.2 copy-start.11
  115.8 2.5 copy-start.13
  118.3 1.4 copy-start.3
  125.5 31.8 %copy-start.10 = (bf16[1,32,4,32,128]{4,3,2,1,0:T(8,128)(2,1)S(1)}, bf16[1,32,4,32,128]{4,3,2,1,0:T(8,128)(2,1)}, u32[]{:S(2)}) copy-start(bf16[1,32,4,32,128]{4,3,2,1,0:T(8,128)(2,1)} %copy.33) | copy-start | bytes 3145732
  157.7 5.9 %copy-start.8 = (bf16[1,32,4,32,128]{4,3,2,1,0:T(8,128)(2,1)S(1)}, bf16[1,32,4,32,128]{4,3,2,1,0:T(8,128)(2,1)}, u32[]{:S(2)}) copy-start(bf16[1,32,4,32,128]{4,3,2,1,0:T(8,128)(2,1)} %copy-done.7) | copy-start | bytes 3145732
  159.4 29.6 %all-to-all-start.3 = ((bf16[1,32,128,128]{3,1,0,2:T(8,128)(2,1)}), bf16[1,32,128,128]{3,1,0,2:T(8,128)(2,1)}, u32[]{:S(2)}, u32[]{:S(2)}) async-start(bf16[1,32,128,128]{3,1,0,2:T(8,128)(2,1)} %copy.38), calls=%async_computation.3 | async-start | bytes 2097152 | tf_op jit(solution)/shard_map/all_to_all | solution.py:108
  164.2 29.1 %copy-start.4 = (f32[4096,128]{1,0:T(8,128)S(1)}, f32[4096,128]{1,0:T(8,128)}, u32[]{:S(2)}) copy-start(f32[4096,128]{1,0:T(8,128)} %copy-done.3) | copy-start | bytes 6291460
  189.0 29.6 %all-to-all-start.4 = ((bf16[1,32,128,128]{3,1,0,2:T(8,128)(2,1)}), bf16[1,32,128,128]{3,1,0,2:T(8,128)(2,1)}, u32[]{:S(2)}, u32[]{:S(2)}) async-start(bf16[1,32,128,128]{3,1,0,2:T(8,128)(2,1)} %copy.41), calls=%async_computation.4 | async-start | bytes 2097152 | tf_op jit(solution)/shard_map/all_to_all | solution.py:109
  193.2 173.5 %all-reduce.4.cloned.1.call-start = ((), (), s32[]{:S(2)}) async-start(), calls=%async_computation.5 | async-start | bytes 786432 | tf_op jit(solution)/shard_map/psum | solution.py:134
  193.9 2.8 copy-start.6
  193.9 2.8 copy-start.12
  218.6 1.9 copy-start.14
  226.8 1.0 copy-start.17
  226.8 1.3 copy-start.18
  226.8 1.6 copy-start.19
  226.8 2.0 copy-start.20
Sparse Core Ops, SparseCore 0:
  237.7 129.0 all-reduce.3
